TPU v7x, 256 devices: a whole 4x4x8 slice. The times are simulated.
256 devices in a mesh: space: 8 (over z_lo, y), vec: 32 (over x, z_hi, core).
Axes of the slice: x: 4, y: 4, z: 8 (z_hi: 4, z_lo: 2; z = z_hi * 2 + z_lo), core: 2. Of those that a mesh axis runs over, the one named last changes fastest.
Arguments:
- vectors: float32 [2, 3, 128, 8, 4096], P(None, None, 'vec', 'space'), may hold values from -6 to 6
- gauge_links: float32 [3, 2, 3, 3, 8, 4096], P(None, None, None, None, 'space'), may hold values from -2.5 to 2.5
- momenta: int32 [2, 3], replicated, may hold values from 1 to 2
- displacements: int32 [2], replicated, may hold values from 0 to 5
Outputs:
- elementals: float32 [2, 4, 128, 128], P(None, None, 'vec', 'space')
All inputs are finite; a program needn't handle non-finite values.
Results may differ from a plain program's by a relative error of at most 0.0003.
Values sent between devices are 32-bit elements; how exact they have to be, the bound alone decides.
No kernel may reach another device: no remote copies, remote signals or barrier semaphores. Data moves between devices by JAX's collectives and lax.ppermute only.
A program may use at most 128 MiB of HBM per device.

v0:
```python
import math
import jax
import jax.numpy as jnp
from jax import lax
from jax.sharding import PartitionSpec as P

NY = 64
NZ = 64
NMOM = 2
NDISP = 2


def extended(block, sides, width):
    for axis, dim in sides:
        count = lax.axis_size(axis)
        forward = [(i, i + 1) for i in range(count - 1)]
        forward.append((count - 1, 0))
        backward = [(target, source) for source, target in forward]
        low = lax.ppermute(
            lax.slice_in_dim(block, block.shape[dim] - width, None, axis=dim), axis, forward
        )
        high = lax.ppermute(lax.slice_in_dim(block, 0, width, axis=dim), axis, backward)
        block = jnp.concatenate([low, block, high], axis=dim)
    return block


def shifted(block, axis, distance):
    devices = range(lax.axis_size(axis))
    route = [((i - distance) % len(devices), i) for i in devices]
    return lax.ppermute(block, axis, route)


def colour_term(gauge_one, colour_field, colour, dagger):
    if dagger:
        link_re = gauge_one[0][colour][:, None]
        link_im = -gauge_one[1][colour][:, None]
    else:
        link_re = gauge_one[0][:, colour][:, None]
        link_im = gauge_one[1][:, colour][:, None]
    vec_re = colour_field[0][colour][None]
    vec_im = colour_field[1][colour][None]
    return (link_re * vec_re - link_im * vec_im, link_re * vec_im + link_im * vec_re)


def link_times(gauge_one, colour_field, dagger):
    real_sum, imag_sum = colour_term(gauge_one, colour_field, 0, dagger)
    for colour in (1, 2):
        real_next, imag_next = colour_term(gauge_one, colour_field, colour, dagger)
        real_sum = real_sum + real_next
        imag_sum = imag_sum + imag_next
    return jnp.stack([real_sum, imag_sum])


def roll_depth(colour_field, offset, row_len):
    total_len = colour_field.shape[-1]
    position = lax.broadcasted_iota(jnp.int32, (total_len,), 0) % row_len
    if offset > 0:
        inner_roll = jnp.roll(colour_field, -1, -1)
        outer_roll = jnp.roll(colour_field, row_len - 1, -1)
        return jnp.where(position == row_len - 1, outer_roll, inner_roll)
    inner_roll = jnp.roll(colour_field, 1, -1)
    outer_roll = jnp.roll(colour_field, 1 - row_len, -1)
    return jnp.where(position == 0, outer_roll, inner_roll)


def plane_pair(colour_field):
    padded = extended(colour_field, (("space", 3),), 1)
    return (padded[:, :, :, 2:], padded[:, :, :, :-2])


def slab_neighbours(colour_field):
    return (
        plane_pair(colour_field),
        (jnp.roll(colour_field, -NZ, 4), jnp.roll(colour_field, NZ, 4)),
        (roll_depth(colour_field, 1, NZ), roll_depth(colour_field, -1, NZ)),
    )


def six_hops(gauge_sites, gauge_back, neighbours):
    forward = [
        link_times(gauge_sites[direction], neighbours[direction][0], False)
        for direction in range(3)
    ]
    backward = [
        link_times(gauge_back[direction], neighbours[direction][1], True) for direction in range(3)
    ]
    return forward + backward


def hopping_sum(hop_list):
    running = hop_list[0]
    for hop_index in range(1, 6):
        running = running + hop_list[hop_index]
    return running


def pair_sums(left_side, right_side):
    hig = lax.Precision.HIGHEST
    real_part = jnp.einsum(
        "cixs,cjxs->ij", left_side[0], right_side[0], precision=hig
    ) + jnp.einsum("cixs,cjxs->ij", left_side[1], right_side[1], precision=hig)
    imag_part = jnp.einsum(
        "cixs,cjxs->ij", left_side[0], right_side[1], precision=hig
    ) - jnp.einsum("cixs,cjxs->ij", left_side[1], right_side[0], precision=hig)
    return (real_part, imag_part)


def local(vectors, gauge_links, momenta, displacements):
    planes = vectors.shape[3]
    global_planes = planes * lax.axis_size("space")
    edge_plane = shifted(gauge_links[0], "space", 1)
    back_plane = jnp.concatenate([edge_plane, gauge_links[0][:, :, :, :-1, :]], 3)
    back_row = jnp.roll(gauge_links[1], NZ, 4)
    back_depth = roll_depth(gauge_links[2], -1, NZ)
    gauge_back = jnp.stack([back_plane, back_row, back_depth])
    first_step = hopping_sum(six_hops(gauge_links, gauge_back, slab_neighbours(vectors))) / -6.0
    filtered = (
        hopping_sum(six_hops(gauge_links, gauge_back, slab_neighbours(first_step))) / -3.0 - vectors
    )
    slab_hops = jnp.stack(six_hops(gauge_links, gauge_back, slab_neighbours(filtered)))
    chosen = [
        lax.dynamic_index_in_dim(slab_hops, displacements[op_index], 0, False)
        for op_index in range(NDISP)
    ]
    exchanged = lax.all_to_all(
        jnp.stack([filtered] + chosen), "vec", split_axis=5, concat_axis=3, tiled=True
    )
    block_field = exchanged[0]
    displaced = [exchanged[1 + op_index] for op_index in range(NDISP)]
    block_len = block_field.shape[4]
    plane_index = lax.axis_index("space") * planes + jnp.arange(planes, dtype=jnp.int32)
    flat_index = lax.axis_index("vec") * block_len + jnp.arange(block_len, dtype=jnp.int32)
    row_index = flat_index // NZ
    depth_index = flat_index % NZ
    real_rows = []
    imag_rows = []
    for op_index in range(NMOM):
        phase_plane = (momenta[op_index, 0] * plane_index % global_planes).astype(
            jnp.float32
        ) / global_planes
        phase_row = (momenta[op_index, 1] * row_index % NY).astype(jnp.float32) / NY
        phase_depth = (momenta[op_index, 2] * depth_index % NZ).astype(jnp.float32) / NZ
        angle_grid = (phase_plane[:, None] + phase_row[None, :] + phase_depth[None, :]) * (
            2.0 * math.pi
        )
        cosine = jnp.cos(angle_grid)
        sine_part = jnp.sin(angle_grid)
        phased = jnp.stack(
            [
                cosine * block_field[0] - sine_part * block_field[1],
                cosine * block_field[1] + sine_part * block_field[0],
            ]
        )
        real_part, imag_part = pair_sums(block_field, phased)
        real_rows.append(real_part)
        imag_rows.append(imag_part)
    for op_index in range(NDISP):
        real_part, imag_part = pair_sums(block_field, displaced[op_index])
        real_rows.append(real_part)
        imag_rows.append(imag_part)
    partial_sums = jnp.stack([jnp.stack(real_rows), jnp.stack(imag_rows)])
    share_sums = lax.psum_scatter(partial_sums, "vec", scatter_dimension=2, tiled=True)
    whole_sums = lax.psum_scatter(share_sums, "space", scatter_dimension=3, tiled=True)
    norm_scale = 1.0 / math.sqrt(3 * global_planes * NY * NZ)
    return whole_sums * norm_scale


def solution(mesh):
    placed = (
        P(None, None, "vec", "space", None),
        P(None, None, None, None, "space", None),
        P(),
        P(),
    )
    return jax.shard_map(
        local, mesh=mesh, in_specs=placed, out_specs=P(None, None, "vec", "space"), check_vma=False
    )
```

profile of v0, /device:TPU:2, one launch (start us, length us, event | category | flops | bytes accessed | tf_op | source)
XLA Modules:
  0.0 637.9 jit_solution(12803463155827763475)
XLA Ops:
  6.5 1.6 collective-permute-start.2
  8.1 2.8 collective-permute-start
  10.9 1.9 slice_bitcast_fusion.1
  12.8 2.1 fusion.117
  15.0 0.9 fusion.120
  15.9 0.9 fusion.123
  17.9 3.8 broadcast_select_fusion.2
  22.7 0.7 broadcast_select_fusion.6
  23.9 0.7 fusion.62
  24.8 0.9 fusion.52
  26.9 1.1 add_bitcast_fusion.15
  28.1 1.1 add_bitcast_fusion.19
  29.2 1.1 add_bitcast_fusion.21
  30.3 1.9 add_bitcast_fusion.13
  32.2 0.7 fusion.132
  36.1 0.8 copy.552
  37.0 0.8 copy.553
  37.8 0.8 copy.554
  38.7 0.8 copy.555
  39.5 0.8 copy.557
  41.7 1.1 fusion.126
  43.0 1.0 fusion.118
  44.3 1.0 fusion.124
  45.7 1.3 add_bitcast_fusion.17
  47.0 1.1 add_bitcast_fusion.23
  48.1 1.9 fusion.18
  50.0 0.8 fusion.19
  50.8 4.1 collective-permute-start.3
  54.9 0.9 fusion.107
  55.9 0.9 fusion.110
  56.8 0.9 fusion.113
  59.2 0.9 broadcast_select_fusion.4
  60.4 0.9 fusion.42
  61.6 0.9 broadcast_select_fusion.1
  62.9 1.1 add_bitcast_fusion.9
  64.0 1.1 add_bitcast_fusion.7
  65.1 1.1 add_bitcast_fusion.3
  66.3 1.1 add_bitcast_fusion.1
  67.8 2.8 collective-permute-done.4
  70.9 1.1 add_bitcast_fusion.11
  72.0 1.3 add_bitcast_fusion.5
  73.3 2.2 fusion.30
  76.1 0.9 fusion.98
  77.0 0.9 fusion.99
  78.0 0.9 fusion.102
  79.1 4.1 collective-permute-start.5
  83.2 0.9 broadcast_select_fusion
  84.5 0.9 fusion.32
  85.7 0.9 broadcast_select_fusion.3
  89.2 1.0 collective-permute-done.6
  92.7 33.3 %copy.147 = f32[3,2,3,4,1,4096]{3,2,4,1,0,5:T(4,128)} copy(f32[3,2,3,4,1,4096]{5,3,2,1,4,0:T(4,128)S(1)} %pad_maximum_fusion) | data formatting | bytes 2359296 | tf_op jit(solution)/shard_map/stack | solution.py:126
  126.0 40.0 %reshape.3120 = f32[32,1,9216]{2,1,0:T(1,128)} reshape(f32[4096,3,2,1,3,4]{5,4,3,2,1,0:T(4,128)} %bitcast.634) | data formatting | bytes 2359296
  166.0 11.0 %all-to-all-start = ((f32[32,1,9216]{2,1,0:T(1,128)}), f32[32,1,9216]{2,1,0:T(1,128)S(1)}, u32[]{:S(2)}, u32[]{:S(2)}) async-start(f32[32,1,9216]{2,1,0:T(1,128)} %reshape.3120), calls=%async_computation | async-start | bytes 2359296 | tf_op jit(solution)/shard_map/all_to_all | solution.py:125
  179.3 2.7 fusion.92
  182.0 25.1 %all-to-all-done = f32[32,1,9216]{2,1,0:T(1,128)S(1)} async-done(((f32[32,1,9216]{2,1,0:T(1,128)}), f32[32,1,9216]{2,1,0:T(1,128)S(1)}, u32[]{:S(2)}, u32[]{:S(2)}) %all-to-all-start) | async-done | bytes 1179680 | tf_op jit(solution)/shard_map/all_to_all | solution.py:125
  207.6 3.4 reduce
  211.1 50.4 %reshape.3121 = f32[4096,3,2,1,3,4]{5,4,3,2,1,0:T(4,128)} reshape(f32[32,9216]{1,0:T(8,128)S(1)} %reduce) | data formatting | bytes 2359296
  261.5 36.2 %copy.148 = f32[3,2,3,4,1,4096]{5,4,3,2,1,0:T(1,128)S(1)} copy(f32[3,2,3,4,1,4096]{3,2,4,1,0,5:T(4,128)} %bitcast.635) | data formatting | bytes 2359296 | tf_op jit(solution)/shard_map/all_to_all | solution.py:125
  305.6 0.8 pad_maximum_fusion.1
  307.7 268.2 %all-reduce.3.cloned.1.call-done = f32[2,4,128,128]{3,2,1,0:T(8,128)} async-done(((f32[2,4,128,128]{3,2,1,0:T(8,128)}), f32[2,4,128,128]{3,2,1,0:T(8,128)}) %all-reduce.3.cloned.1.call-update) | async-done | bytes 524304
  575.9 0.8 constant_dynamic-slice_fusion
  577.0 1.0 reshape.3117
  577.9 51.2 %reduce-scatter.5.cloned.1.call-done = f32[16,32]{1,0:T(8,128)} async-done(((f32[128,32]{1,0:T(8,128)}), f32[16,32]{1,0:T(8,128)}) %reduce-scatter.5.cloned.1.call-update) | async-done | bytes 2064
  629.1 0.8 reshape.3118
  (230 shorter events, 25.5 us)
Async XLA Ops:
  6.5 8.4 %copy-start = (f32[2,3,4,1,4096]{4,3,2,1,0:T(1,128)S(1)}, f32[2,3,4,1,4096]{4,3,2,1,0:T(1,128)}, u32[]{:S(2)}) copy-start(f32[2,3,4,1,4096]{4,3,2,1,0:T(1,128)} %param.4) | copy-start | bytes 1179652
  6.5 36.5 %collective-permute-start.2 = (f32[2,3,4,1,4096]{4,3,2,1,0:T(1,128)}, f32[2,3,4,1,4096]{4,3,2,1,0:T(1,128)}, u32[]{:S(2)}, u32[]{:S(2)}) collective-permute-start(f32[2,3,4,1,4096]{4,3,2,1,0:T(1,128)} %param.4), channel_id=1, source_target_pairs={{0,32},{32,64},{64,96},{96,128},{128,160},{160,192},{192,224},{224... | collective-permute-start | bytes 1179656 | tf_op jit(solution)/shard_map/ppermute | solution.py:19
  8.1 36.2 %collective-permute-start = (f32[2,3,4,1,4096]{4,3,2,1,0:T(1,128)}, f32[2,3,4,1,4096]{4,3,2,1,0:T(1,128)}, u32[]{:S(2)}, u32[]{:S(2)}) collective-permute-start(f32[2,3,4,1,4096]{4,3,2,1,0:T(1,128)} %param.4), channel_id=1, source_target_pairs={{32,0},{64,32},{96,64},{128,96},{160,128},{192,160},{224,192},{0,2... | collective-permute-start | bytes 1179656 | tf_op jit(solution)/shard_map/ppermute | solution.py:22
  12.8 4.2 copy-start.1
  12.8 28.8 %collective-permute-start.1 = (f32[2,3,3,1,4096]{4,3,2,1,0:T(1,128)}, f32[2,3,3,1,4096]{4,3,2,1,0:T(1,128)}, u32[]{:S(2)}, u32[]{:S(2)}) collective-permute-start(f32[2,3,3,1,4096]{4,3,2,1,0:T(1,128)} %get-tuple-element.24), channel_id=1, source_target_pairs={{224,0},{0,32},{32,64},{64,96},{96,128},{128,160},{160,192},{192,2... | collective-permute-start | bytes 884744 | tf_op jit(solution)/shard_map/ppermute | solution.py:30
  28.1 4.8 copy-start.5
  45.6 4.4 copy-start.2
  45.7 4.4 copy-start.3
  50.8 16.6 %collective-permute-start.3 = (f32[2,3,4,1,4096]{4,3,2,1,0:T(1,128)S(1)}, f32[2,3,4,1,4096]{4,3,2,1,0:T(1,128)S(1)}, u32[]{:S(2)}, u32[]{:S(2)}) collective-permute-start(f32[2,3,4,1,4096]{4,3,2,1,0:T(1,128)S(1)} %fusion.19), channel_id=1, source_target_pairs={{32,0},{64,32},{96,64},{128,96},{160,128},{192,160},{224,192},{0,2... | collective-permute-start | bytes 1179656 | tf_op jit(solution)/shard_map/ppermute | solution.py:22
  57.8 12.7 %collective-permute-start.4 = (f32[2,3,4,1,4096]{4,3,2,1,0:T(1,128)S(1)}, f32[2,3,4,1,4096]{4,3,2,1,0:T(1,128)S(1)}, u32[]{:S(2)}, u32[]{:S(2)}) collective-permute-start(f32[2,3,4,1,4096]{4,3,2,1,0:T(1,128)S(1)} %fusion.19), channel_id=1, source_target_pairs={{0,32},{32,64},{64,96},{96,128},{128,160},{160,192},{192,224},{224... | collective-permute-start | bytes 1179656 | tf_op jit(solution)/shard_map/ppermute | solution.py:19
  79.0 11.3 %collective-permute-start.6 = (f32[2,3,4,1,4096]{4,3,2,1,0:T(1,128)S(1)}, f32[2,3,4,1,4096]{4,3,2,1,0:T(1,128)S(1)}, u32[]{:S(2)}, u32[]{:S(2)}) collective-permute-start(f32[2,3,4,1,4096]{4,3,2,1,0:T(1,128)S(1)} %copy_subtract_fusion), channel_id=1, source_target_pairs={{0,32},{32,64},{64,96},{96,128},{128,160},{160,192},{192,224},{224... | collective-permute-start | bytes 1179656 | tf_op jit(solution)/shard_map/ppermute | solution.py:19
  79.1 11.5 %collective-permute-start.5 = (f32[2,3,4,1,4096]{4,3,2,1,0:T(1,128)S(1)}, f32[2,3,4,1,4096]{4,3,2,1,0:T(1,128)S(1)}, u32[]{:S(2)}, u32[]{:S(2)}) collective-permute-start(f32[2,3,4,1,4096]{4,3,2,1,0:T(1,128)S(1)} %copy_subtract_fusion), channel_id=1, source_target_pairs={{32,0},{64,32},{96,64},{128,96},{160,128},{192,160},{224,192},{0,2... | collective-permute-start | bytes 1179656 | tf_op jit(solution)/shard_map/ppermute | solution.py:22
  166.0 11.2 %copy-start.4 = (s32[2,3]{1,0:T(2,128)S(1)}, s32[2,3]{1,0:T(2,128)}, u32[]{:S(2)}) copy-start(s32[2,3]{1,0:T(2,128)} %param.6) | copy-start | bytes 76
  166.0 41.1 %all-to-all-start = ((f32[32,1,9216]{2,1,0:T(1,128)}), f32[32,1,9216]{2,1,0:T(1,128)S(1)}, u32[]{:S(2)}, u32[]{:S(2)}) async-start(f32[32,1,9216]{2,1,0:T(1,128)} %reshape.3120), calls=%async_computation | async-start | bytes 2359296 | tf_op jit(solution)/shard_map/all_to_all | solution.py:125
  177.0 398.9 %all-reduce.3.cloned.1.call-start = ((), (), s32[]{:S(2)}) async-start(), calls=%async_computation.3 | async-start | bytes 1048576
  303.9 2.5 copy-start.6
  306.4 322.7 %reduce-scatter.5.cloned.1.call-start = ((), (), s32[]{:S(2)}) async-start(), calls=%async_computation.2 | async-start | bytes 73728
Sparse Core Ops, SparseCore 0:
  306.5 269.3 all-reduce.2
  578.5 50.5 reduce-scatter.4
where the time goes:
time: 646 us; the launch traced here: 638 us
  waiting for transfers between devices  348 us (54%)
  local copies, waits for them, and re-layouts  193 us (30%)
  other arithmetic  44.6 us (7%)
  starting transfers between devices  24.5 us (4%)
  between operations  21.3 us (3%)
    unnamed x4, waiting for transfers between devices  319 us
    unnamed x146, local copies, waits for them, and re-layouts  104 us
    all_to_all x2, local copies, waits for them, and re-layouts, local(): lax.all_to_all(jnp.stack([filtered] + chosen), 'vec', split_axis=5, conca...  36.7 us
    another operation x1, local copies, waits for them, and re-layouts, local(): jnp.stack([filtered] + chosen)  33.3 us
    all_to_all x1, waiting for transfers between devices, local(): lax.all_to_all(jnp.stack([filtered] + chosen), 'vec', split_axis=5, conca...  25.1 us
    another operation x12, other arithmetic, link_times(): return jnp.stack([real_sum, imag_sum])  14.6 us
  transfers between devices with their start and end apart: 10, of which 5 were waited for; matrix products, arithmetic and copies ran while one was open for 8% of the time, Pallas kernels for 0%

commit v1 on v0

--- a/solution.py
+++ b/solution.py
@@ -122,8 +122,14 @@
         lax.dynamic_index_in_dim(slab_hops, displacements[op_index], 0, False)
         for op_index in range(NDISP)
     ]
-    exchanged = lax.all_to_all(
-        jnp.stack([filtered] + chosen), "vec", split_axis=5, concat_axis=3, tiled=True
+    exchanged = jnp.concatenate(
+        lax.all_to_all(
+            jnp.stack(jnp.split(jnp.stack([filtered] + chosen), lax.axis_size("vec"), axis=5)),
+            "vec",
+            0,
+            0,
+        ),
+        axis=3,
     )
     block_field = exchanged[0]
     displaced = [exchanged[1 + op_index] for op_index in range(NDISP)]

time: 646 us -> 472 us (0.73)
  local copies, waits for them, and re-layouts: 193 us -> 41.9 us
  other arithmetic: 44.6 us -> 19.3 us
  waiting for transfers between devices: 348 us -> 357 us
    unnamed x146 -> x98, local copies, waits for them, and re-layouts: 104 us -> 27.4 us
    all_to_all x2 -> x1, local copies, waits for them, and re-layouts: 36.7 us -> 0.21 us  [local(): lax.all_to_all(jnp.stack(jnp.split(jnp.stack([filtered] + chosen), lax.ax...]
    another operation x1, local copies, waits for them, and re-layouts: 33.3 us -> 0.61 us  [local(): jnp.stack(jnp.split(jnp.stack([filtered] + chosen), lax.axis_size('vec'),...]
    another operation x12, other arithmetic: 14.6 us -> 4.19 us  [link_times(): return jnp.stack([real_sum, imag_sum])]
  transfers between devices with their start and end apart: 10 -> 10, of which waited for: 5 -> 5; matrix products, arithmetic and copies ran while one was open for 8% -> 6% of each run, Pallas kernels for 0% -> 0%
where the time goes in v1:
time: 472 us; the launch traced here: 469 us
  waiting for transfers between devices  357 us (76%)
  local copies, waits for them, and re-layouts  41.9 us (9%)
  starting transfers between devices  24.4 us (5%)
  between operations  20.2 us (4%)
  other arithmetic  19.3 us (4%)
  matrix products  6.2 us (1%)
    unnamed x4, waiting for transfers between devices  320 us
    unnamed x98, local copies, waits for them, and re-layouts  27.4 us
    all_to_all x1, waiting for transfers between devices, local(): lax.all_to_all(jnp.stack(jnp.split(jnp.stack([filtered] + chosen), lax.ax...  25.6 us
    all_to_all x1, starting transfers between devices, local(): lax.all_to_all(jnp.stack(jnp.split(jnp.stack([filtered] + chosen), lax.ax...  10.9 us
    ppermute x3, starting transfers between devices, extended(): lax.ppermute(lax.slice_in_dim(block, 0, width, axis=dim), axis, backward)  9.81 us
  transfers between devices with their start and end apart: 10, of which 5 were waited for; matrix products, arithmetic and copies ran while one was open for 6% of the time, Pallas kernels for 0%

profile of v1, /device:TPU:2, one launch (start us, length us, event | category | flops | bytes accessed | tf_op | source)
XLA Modules:
  0.0 469.1 jit_solution(110087936946280246)
XLA Ops:
  6.5 1.6 collective-permute-start.2
  8.1 2.8 collective-permute-start
  10.9 1.9 slice_bitcast_fusion
  13.3 0.7 slice.1531
  14.1 0.9 fusion.140
  15.0 0.9 fusion.139
  16.0 0.9 fusion.143
  17.1 0.7 broadcast_select_fusion
  20.6 0.7 fusion.90
  21.5 0.9 fusion.36
  24.3 1.0 add_bitcast_fusion.19
  25.3 0.6 fusion.152
  29.1 0.8 copy.441
  31.2 1.1 fusion.147
  32.5 1.0 fusion.144
  33.8 1.0 fusion.145
  37.8 0.8 collective-permute-start.4
  38.6 3.4 collective-permute-start.3
  44.3 6.3 %collective-permute-done.4 = f32[2,3,4,1,4096]{4,2,1,0,3:T(4,128)S(1)} collective-permute-done((f32[2,3,4,1,4096]{4,2,1,0,3:T(4,128)S(1)}, f32[2,3,4,1,4096]{4,2,1,0,3:T(4,128)S(1)}, u32[]{:S(2)}, u32[]{:S(2)}) %collective-permute-start.4) | collective-permute-done | bytes 393248 | tf_op jit(solution)/shard_map/ppermute | solution.py:19
  51.2 0.7 fusion.188
  51.9 0.7 fusion.28
  53.7 0.7 collective-permute-start.6
  54.4 3.6 collective-permute-start.5
  60.2 4.7 %collective-permute-done.5 = f32[2,3,4,1,4096]{4,2,1,0,3:T(4,128)S(1)} collective-permute-done((f32[2,3,4,1,4096]{4,2,1,0,3:T(4,128)S(1)}, f32[2,3,4,1,4096]{4,2,1,0,3:T(4,128)S(1)}, u32[]{:S(2)}, u32[]{:S(2)}) %collective-permute-start.5) | collective-permute-done | bytes 393248 | tf_op jit(solution)/shard_map/ppermute | solution.py:22
  67.0 0.6 constant_dynamic-update-slice_fusion.31
  67.6 0.6 constant_dynamic-update-slice_fusion.30
  68.2 0.6 constant_dynamic-update-slice_fusion.29
  68.9 0.6 constant_dynamic-update-slice_fusion.28
  69.5 0.6 constant_dynamic-update-slice_fusion.27
  70.1 0.6 constant_dynamic-update-slice_fusion.26
  70.7 0.6 constant_dynamic-update-slice_fusion.25
  71.3 0.6 constant_dynamic-update-slice_fusion.24
  71.9 0.6 constant_dynamic-update-slice_fusion.23
  73.2 0.6 constant_dynamic-update-slice_fusion.21
  73.8 0.6 constant_dynamic-update-slice_fusion.20
  74.4 0.6 constant_dynamic-update-slice_fusion.19
  75.6 0.6 constant_dynamic-update-slice_fusion.17
  76.2 0.6 constant_dynamic-update-slice_fusion.16
  76.9 0.6 constant_dynamic-update-slice_fusion.15
  77.5 0.6 constant_dynamic-update-slice_fusion.14
  78.1 0.6 constant_dynamic-update-slice_fusion.13
  78.7 0.6 constant_dynamic-update-slice_fusion.12
  79.9 0.6 constant_dynamic-update-slice_fusion.10
  80.5 0.6 constant_dynamic-update-slice_fusion.9
  81.2 0.6 constant_dynamic-update-slice_fusion.8
  81.8 0.6 constant_dynamic-update-slice_fusion.7
  82.4 0.6 constant_dynamic-update-slice_fusion.6
  83.0 0.6 constant_dynamic-update-slice_fusion.5
  83.6 0.6 constant_dynamic-update-slice_fusion.4
  84.2 0.6 constant_dynamic-update-slice_fusion.3
  84.8 0.6 constant_dynamic-update-slice_fusion.2
  85.5 0.6 constant_dynamic-update-slice_fusion.1
  86.1 0.6 constant_dynamic-update-slice_fusion
  86.7 10.9 %all-to-all-start = ((f32[32,3,2,3,4,1,128]{6,5,4,3,2,1,0:T(1,128)}), f32[32,3,2,3,4,1,128]{6,5,4,3,2,1,0:T(1,128)S(1)}, u32[]{:S(2)}, u32[]{:S(2)}) async-start(f32[32,3,2,3,4,1,128]{6,5,4,3,2,1,0:T(1,128)} %constant_dynamic-update-slice_fusion), calls=%async_computation | async-start | bytes 2359296 | tf_op jit(solution)/shard_map/all_to_all | solution.py:126
  97.7 0.6 fusion.154
  99.6 2.4 fusion.120
  102.2 25.6 %all-to-all-done = f32[32,3,2,3,4,1,128]{6,5,4,3,2,1,0:T(1,128)S(1)} async-done(((f32[32,3,2,3,4,1,128]{6,5,4,3,2,1,0:T(1,128)}), f32[32,3,2,3,4,1,128]{6,5,4,3,2,1,0:T(1,128)S(1)}, u32[]{:S(2)}, u32[]{:S(2)}) %all-to-all-start) | async-done | bytes 1179680 | tf_op jit(solution)/shard_map/all_to_all | solution.py:126
  135.9 0.8 pad_maximum_fusion.1
  138.0 269.2 %all-reduce.3.cloned.1.call-done = f32[2,4,128,128]{3,2,1,0:T(8,128)} async-done(((f32[2,4,128,128]{3,2,1,0:T(8,128)}), f32[2,4,128,128]{3,2,1,0:T(8,128)}) %all-reduce.3.cloned.1.call-update) | async-done | bytes 524304
  407.3 0.8 constant_dynamic-slice_fusion
  408.3 1.0 reshape.3122
  409.3 51.2 %reduce-scatter.5.cloned.1.call-done = f32[16,32]{1,0:T(8,128)} async-done(((f32[128,32]{1,0:T(8,128)}), f32[16,32]{1,0:T(8,128)}) %reduce-scatter.5.cloned.1.call-update) | async-done | bytes 2064
  460.5 0.8 reshape.3123
  461.4 0.6 broadcast_multiply_fusion
  (182 shorter events, 28.6 us)
Async XLA Ops:
  6.5 7.5 %copy-start = (f32[2,3,4,1,4096]{4,3,2,1,0:T(1,128)S(1)}, f32[2,3,4,1,4096]{4,3,2,1,0:T(1,128)}, u32[]{:S(2)}) copy-start(f32[2,3,4,1,4096]{4,3,2,1,0:T(1,128)} %param.4) | copy-start | bytes 1179652
  6.5 26.0 %collective-permute-start.2 = (f32[2,3,4,1,4096]{4,3,2,1,0:T(1,128)}, f32[2,3,4,1,4096]{4,3,2,1,0:T(1,128)}, u32[]{:S(2)}, u32[]{:S(2)}) collective-permute-start(f32[2,3,4,1,4096]{4,3,2,1,0:T(1,128)} %param.4), channel_id=1, source_target_pairs={{0,32},{32,64},{64,96},{96,128},{128,160},{160,192},{192,224},{224... | collective-permute-start | bytes 1179656 | tf_op jit(solution)/shard_map/ppermute | solution.py:19
  8.1 25.7 %collective-permute-start = (f32[2,3,4,1,4096]{4,3,2,1,0:T(1,128)}, f32[2,3,4,1,4096]{4,3,2,1,0:T(1,128)}, u32[]{:S(2)}, u32[]{:S(2)}) collective-permute-start(f32[2,3,4,1,4096]{4,3,2,1,0:T(1,128)} %param.4), channel_id=1, source_target_pairs={{32,0},{64,32},{96,64},{128,96},{160,128},{192,160},{224,192},{0,2... | collective-permute-start | bytes 1179656 | tf_op jit(solution)/shard_map/ppermute | solution.py:22
  12.8 18.3 %collective-permute-start.1 = (f32[2,3,3,1,4096]{4,3,2,1,0:T(1,128)}, f32[2,3,3,1,4096]{4,3,2,1,0:T(1,128)}, u32[]{:S(2)}, u32[]{:S(2)}) collective-permute-start(f32[2,3,3,1,4096]{4,3,2,1,0:T(1,128)} %get-tuple-element.56), channel_id=1, source_target_pairs={{224,0},{0,32},{32,64},{64,96},{96,128},{128,160},{160,192},{192,2... | collective-permute-start | bytes 884744 | tf_op jit(solution)/shard_map/ppermute | solution.py:30
  15.8 1.2 copy-start.1
  24.3 1.7 copy-start.5
  35.3 0.9 copy-start.2
  35.3 1.0 copy-start.3
  37.8 12.7 %collective-permute-start.4 = (f32[2,3,4,1,4096]{4,2,1,0,3:T(4,128)S(1)}, f32[2,3,4,1,4096]{4,2,1,0,3:T(4,128)S(1)}, u32[]{:S(2)}, u32[]{:S(2)}) collective-permute-start(f32[2,3,4,1,4096]{4,2,1,0,3:T(4,128)S(1)} %fusion.21), channel_id=1, source_target_pairs={{0,32},{32,64},{64,96},{96,128},{128,160},{160,192},{192,224},{224... | collective-permute-start | bytes 1179656 | tf_op jit(solution)/shard_map/ppermute | solution.py:19
  38.6 12.2 %collective-permute-start.3 = (f32[2,3,4,1,4096]{4,2,1,0,3:T(4,128)S(1)}, f32[2,3,4,1,4096]{4,2,1,0,3:T(4,128)S(1)}, u32[]{:S(2)}, u32[]{:S(2)}) collective-permute-start(f32[2,3,4,1,4096]{4,2,1,0,3:T(4,128)S(1)} %fusion.21), channel_id=1, source_target_pairs={{32,0},{64,32},{96,64},{128,96},{160,128},{192,160},{224,192},{0,2... | collective-permute-start | bytes 1179656 | tf_op jit(solution)/shard_map/ppermute | solution.py:22
  53.7 11.9 %collective-permute-start.6 = (f32[2,3,4,1,4096]{4,2,1,0,3:T(4,128)S(1)}, f32[2,3,4,1,4096]{4,2,1,0,3:T(4,128)S(1)}, u32[]{:S(2)}, u32[]{:S(2)}) collective-permute-start(f32[2,3,4,1,4096]{4,2,1,0,3:T(4,128)S(1)} %fusion.28), channel_id=1, source_target_pairs={{0,32},{32,64},{64,96},{96,128},{128,160},{160,192},{192,224},{224... | collective-permute-start | bytes 1179656 | tf_op jit(solution)/shard_map/ppermute | solution.py:19
  54.4 10.5 %collective-permute-start.5 = (f32[2,3,4,1,4096]{4,2,1,0,3:T(4,128)S(1)}, f32[2,3,4,1,4096]{4,2,1,0,3:T(4,128)S(1)}, u32[]{:S(2)}, u32[]{:S(2)}) collective-permute-start(f32[2,3,4,1,4096]{4,2,1,0,3:T(4,128)S(1)} %fusion.28), channel_id=1, source_target_pairs={{32,0},{64,32},{96,64},{128,96},{160,128},{192,160},{224,192},{0,2... | collective-permute-start | bytes 1179656 | tf_op jit(solution)/shard_map/ppermute | solution.py:22
  86.7 11.0 %copy-start.4 = (s32[2,3]{1,0:T(2,128)S(1)}, s32[2,3]{1,0:T(2,128)}, u32[]{:S(2)}) copy-start(s32[2,3]{1,0:T(2,128)} %param.6) | copy-start | bytes 76
  86.7 41.1 %all-to-all-start = ((f32[32,3,2,3,4,1,128]{6,5,4,3,2,1,0:T(1,128)}), f32[32,3,2,3,4,1,128]{6,5,4,3,2,1,0:T(1,128)S(1)}, u32[]{:S(2)}, u32[]{:S(2)}) async-start(f32[32,3,2,3,4,1,128]{6,5,4,3,2,1,0:T(1,128)} %constant_dynamic-update-slice_fusion), calls=%async_computation | async-start | bytes 2359296 | tf_op jit(solution)/shard_map/all_to_all | solution.py:126
  97.6 309.6 %all-reduce.3.cloned.1.call-start = ((), (), s32[]{:S(2)}) async-start(), calls=%async_computation.3 | async-start | bytes 1048576
  135.8 1.0 copy-start.6
  136.7 323.8 %reduce-scatter.5.cloned.1.call-start = ((), (), s32[]{:S(2)}) async-start(), calls=%async_computation.2 | async-start | bytes 73728
Sparse Core Ops, SparseCore 0:
  136.9 270.3 all-reduce.2
  409.9 50.5 reduce-scatter.4
